TPU v7x, 32 devices: a whole 2x2x4 slice. The times are simulated.
32 devices in a mesh: gx: 4 (over y, core), gy: 8 (over z, x).
Axes of the slice: x: 2, y: 2, z: 4, core: 2. Of those that a mesh axis runs over, the one named last changes fastest.
Arguments:
- basis: float32 [3, 400, 4, 10240], P(None, None, 'gx', 'gy'), may hold values from -0.3125 to 0.3125
- connectivity: int32 [8, 4, 8192], P(None, 'gx', 'gy'), may hold values from 0 to 1791
- send_nodes: int32 [4, 4, 1024], P(None, 'gx', 'gy'), may hold values from 0 to 1279
- modulus: float32 [4, 8192], P('gx', 'gy'), may hold values from 0.2 to 5
- ecsw_weight: float32 [4, 8192], P('gx', 'gy'), may hold values from 0.3 to 6
- stiffness: float32 [24, 24], replicated, may hold values from -1.25 to 1.25
- coords: float32 [400], replicated, may hold values from -6 to 6
- velocity: float32 [400], replicated, may hold values from -3 to 3
- external: float32 [400], replicated, may hold values from -12 to 12
Outputs:
- final_coords: float32 [400], replicated
- final_velocity: float32 [400], replicated
- reduced_force: float32 [400], replicated
- displaced: float32 [3, 4, 10240], P(None, 'gx', 'gy')
Inputs may be any that keep to these rules, and one draw needn't show every extreme that they name: `connectivity`: entries index a partition's node table: its 1280 owned nodes, then 128 nodes from each of the neighbours below and above along gx, then below and above along gy. `send_nodes`: Owned-node indices of a partition, 128 for each neighbour, in the order below and above along gx, below and above along gy; an index may repeat.
All inputs are finite; a program needn't handle non-finite values.
Results may differ from a plain program's by a relative error of at most 0.0003.
Values sent between devices are 32-bit elements; how exact they have to be, the bound alone decides.
A program may use at most 128 MiB of HBM per device.

v0:
```python
import jax
import jax.numpy as jnp
from jax import lax
from jax.sharding import PartitionSpec as P

STEPS = 2


time_step = 0.05


def with_halo(x, sides, width):
    for axis, dim in sides:
        size, length = (lax.axis_size(axis), x.shape[dim])
        up = [(i, (i + 1) % size) for i in range(size - 1)]
        down = [(j, i) for i, j in up]
        last = lax.slice_in_dim(x, length - width, length, axis=dim)
        first = lax.slice_in_dim(x, 0, width, axis=dim)
        before = lax.ppermute(last, axis, up)
        after = lax.ppermute(first, axis, down)
        x = jnp.concatenate([before, x, after], axis=dim)
    return x


def element_forces(moved, links, stiffness, factor):
    corner = moved[:, links]
    stacked = corner.reshape(24, links.shape[1])
    strain = jnp.dot(stiffness, stacked, precision=lax.Precision.HIGHEST)
    forces = factor * (strain + strain * strain * strain / 3.0)
    return jnp.zeros_like(moved).at[:, links].add(forces.reshape(3, 8, links.shape[1]))


def trade(blocks):
    along_x = with_halo(jnp.stack([blocks[0], blocks[1]]), (("gx", 0),), 1)
    along_y = with_halo(jnp.stack([blocks[2], blocks[3]]), (("gy", 0),), 1)
    return (along_x[0], along_x[3], along_y[0], along_y[3])


def advance(partial_value, coords, velocity, external):
    reduced = lax.psum(partial_value, ("gx", "gy"))
    velocity = velocity + time_step * (external - reduced)
    coords = coords + time_step * velocity
    return (coords, velocity, reduced)


def shards(
    basis, connectivity, send_nodes, modulus, ecsw_weight, stiffness, coords, velocity, external
):
    owned_rows = basis[:, :, 0, :]
    links = connectivity[:, 0, :]
    senders = send_nodes[:, 0, :]
    factor = (modulus * ecsw_weight)[0]
    owned_count = owned_rows.shape[2]
    margin_count = senders.shape[1]
    highest = lax.Precision.HIGHEST
    reduced = jnp.zeros_like(coords)
    for repeat in range(STEPS):
        moved_own = jnp.einsum("ckn,k->cn", owned_rows, coords, precision=highest)
        blocks = tuple((moved_own[:, senders[side]] for side in range(4)))
        moved = jnp.concatenate((moved_own,) + trade(blocks), axis=1)
        nodal = element_forces(moved, links, stiffness, factor)
        margins = tuple(
            (
                nodal[
                    :, owned_count + side * margin_count : owned_count + (side + 1) * margin_count
                ]
                for side in range(4)
            )
        )
        returned = trade(margins)
        owned_force = nodal[:, :owned_count]
        for side in range(4):
            owned_force = owned_force.at[:, senders[side]].add(returned[side])
        partial_value = jnp.einsum("ckn,cn->k", owned_rows, owned_force, precision=highest)
        coords, velocity, reduced = advance(partial_value, coords, velocity, external)
    displaced = jnp.einsum("ckn,k->cn", owned_rows, coords, precision=highest)
    return (coords, velocity, reduced, displaced[:, None, :])


def solution(mesh):
    return jax.shard_map(
        shards,
        mesh=mesh,
        in_specs=(
            P(None, None, "gx", "gy"),
            P(None, "gx", "gy"),
            P(None, "gx", "gy"),
            P("gx", "gy"),
            P("gx", "gy"),
            P(),
            P(),
            P(),
            P(),
        ),
        out_specs=(P(), P(), P(), P(None, "gx", "gy")),
        check_vma=False,
    )
```

profile of v0, /device:TPU:0, one launch (start us, length us, event | category | flops | bytes accessed | tf_op | source)
XLA Modules:
  0.0 347.4 jit_solution(10999625008668332901)
XLA Ops:
  1.4 6.0 %fusion.8 = f32[1,3,1280]{2,0,1:T(1,128)S(1)} fusion(f32[400,1,1]{0,1,2:T(1,128)} %bitcast.207, f32[3,400,1,1280]{3,2,1,0:T(1,128)} %param.9), kind=kOutput, calls=%fused_computation.28 | convolution fusion | flops 18432000 | bytes 6160960 | tf_op jit(solution)/shard_map/ckn,k->cn/dot_general | solution.py:58
  8.3 2.4 collective-permute-start
  13.3 4.2 %collective-permute-start.2 = (f32[1,3,128]{1,2,0:T(8,128)S(1)}, f32[1,3,128]{1,2,0:T(8,128)S(1)}, u32[]{:S(2)}, u32[]{:S(2)}) collective-permute-start(f32[1,3,128]{1,2,0:T(8,128)S(1)} %bitcast.216), channel_id=1, source_target_pairs={{0,1},{1,2},{2,3},{3,4},{4,5},{5,6},{6,7},{8,9},{9,10},{10,11},{11... | collective-permute-start | bytes 4616 | tf_op jit(solution)/shard_map/ppermute | solution.py:19
  19.7 4.6 %collective-permute-done.3 = f32[1,3,128]{1,2,0:T(8,128)S(1)} collective-permute-done((f32[1,3,128]{1,2,0:T(8,128)S(1)}, f32[1,3,128]{1,2,0:T(8,128)S(1)}, u32[]{:S(2)}, u32[]{:S(2)}) %collective-permute-start.3) | collective-permute-done | bytes 1568 | tf_op jit(solution)/shard_map/ppermute | solution.py:20
  24.3 27.7 %gather_fusion.4 = f32[8192,3]{1,0:T(8,128)} fusion(f32[3,1792]{0,1:T(8,128)S(1)} %bitcast_dynamic-update-slice_fusion.4, s32[8192]{0:T(1024)S(1)} %broadcast_clamp_fusion), kind=kCustom, calls=%fused_computation.4 | custom fusion | bytes 229376 | tf_op jit(solution)/shard_map/gather | solution.py:26
  52.0 2.9 copy.35
  55.1 2.6 copy.36
  57.8 44.5 %scatter_custom_fusion = f32[3,1792]{0,1:T(8,128)S(1)} fusion(s32[8192]{0:T(1024)S(1)} %bitcast.201, f32[8192,3]{1,0:T(8,128)} %bitcast.189, f32[]{:T(128)} %constant.6.clone.1), kind=kCustom, calls=%fused_computation.39 | custom fusion | flops 24576 | bytes 22016 | tf_op jit(solution)/shard_map/scatter-add | solution.py:30
  102.4 2.9 collective-permute-start.4
  106.6 4.4 %collective-permute-start.6 = (f32[1,3,128]{1,2,0:T(8,128)S(1)}, f32[1,3,128]{1,2,0:T(8,128)S(1)}, u32[]{:S(2)}, u32[]{:S(2)}) collective-permute-start(f32[1,3,128]{1,2,0:T(8,128)S(1)} %get-tuple-element.11), channel_id=1, source_target_pairs={{0,1},{1,2},{2,3},{3,4},{4,5},{5,6},{6,7},{8,9},{9,10},{10,11},{11... | collective-permute-start | bytes 4616 | tf_op jit(solution)/shard_map/ppermute | solution.py:19
  112.3 1.5 scatter_custom_fusion.1
  113.8 1.5 scatter_custom_fusion.2
  115.4 1.5 scatter_custom_fusion.3
  117.1 1.7 scatter_custom_fusion.4
  119.0 7.8 %fusion.6 = f32[1,400,1]{1,0,2:T(1,128)S(1)} fusion(f32[3,1280,1]{1,2,0:T(1,128)S(1)} %copy.40, f32[3,400,1,1280]{3,2,1,0:T(1,128)} %param.9), kind=kOutput, calls=%fused_computation.26 | convolution fusion | flops 18432000 | bytes 6160960 | tf_op jit(solution)/shard_map/ckn,cn->k/dot_general | solution.py:74
  126.8 45.3 %psum.14 = f32[400]{0:T(512)S(1)} all-reduce(f32[400]{0:T(512)S(1)} %bitcast.209), channel_id=1, replica_groups=mesh['gx'=4,'gy'=8] {'gx','gy'}, use_global_device_ids=true, to_apply=%region_5.0 | all-reduce | flops 400 | bytes 3200 | tf_op jit(solution)/shard_map/psum | solution.py:40
  172.1 5.7 %fusion.4 = f32[1,3,1280]{2,0,1:T(1,128)S(1)} fusion(f32[400,1,1]{0,1,2:T(1,128)S(1)} %bitcast.206, f32[3,400,1,1280]{3,2,1,0:T(1,128)} %param.9), kind=kOutput, calls=%fused_computation.24 | convolution fusion | flops 18432000 | bytes 6160960 | tf_op jit(solution)/shard_map/ckn,k->cn/dot_general | solution.py:58
  183.3 4.2 %collective-permute-start.10 = (f32[1,3,128]{1,2,0:T(8,128)S(1)}, f32[1,3,128]{1,2,0:T(8,128)S(1)}, u32[]{:S(2)}, u32[]{:S(2)}) collective-permute-start(f32[1,3,128]{1,2,0:T(8,128)S(1)} %bitcast.215), channel_id=1, source_target_pairs={{0,1},{1,2},{2,3},{3,4},{4,5},{5,6},{6,7},{8,9},{9,10},{10,11},{11... | collective-permute-start | bytes 4616 | tf_op jit(solution)/shard_map/ppermute | solution.py:19
  189.4 4.3 %collective-permute-done.11 = f32[1,3,128]{1,2,0:T(8,128)S(1)} collective-permute-done((f32[1,3,128]{1,2,0:T(8,128)S(1)}, f32[1,3,128]{1,2,0:T(8,128)S(1)}, u32[]{:S(2)}, u32[]{:S(2)}) %collective-permute-start.11) | collective-permute-done | bytes 1568 | tf_op jit(solution)/shard_map/ppermute | solution.py:20
  193.7 27.7 %gather_fusion.9 = f32[8192,3]{1,0:T(8,128)} fusion(f32[3,1792]{0,1:T(8,128)S(1)} %bitcast_dynamic-update-slice_fusion, s32[8192]{0:T(1024)S(1)} %broadcast_clamp_fusion), kind=kCustom, calls=%fused_computation.9 | custom fusion | bytes 229376 | tf_op jit(solution)/shard_map/gather | solution.py:26
  221.4 2.9 copy.37
  224.5 2.6 copy.38
  227.1 44.5 %scatter_custom_fusion.5 = f32[3,1792]{0,1:T(8,128)S(1)} fusion(s32[8192]{0:T(1024)S(1)} %bitcast.202, f32[8192,3]{1,0:T(8,128)} %bitcast.188, f32[]{:T(128)} %constant.6.clone.1), kind=kCustom, calls=%fused_computation.37 | custom fusion | flops 24576 | bytes 22016 | tf_op jit(solution)/shard_map/scatter-add | solution.py:30
  271.7 2.4 collective-permute-start.12
  275.4 3.9 %collective-permute-start.14 = (f32[1,3,128]{1,2,0:T(8,128)S(1)}, f32[1,3,128]{1,2,0:T(8,128)S(1)}, u32[]{:S(2)}, u32[]{:S(2)}) collective-permute-start(f32[1,3,128]{1,2,0:T(8,128)S(1)} %get-tuple-element.7), channel_id=1, source_target_pairs={{0,1},{1,2},{2,3},{3,4},{4,5},{5,6},{6,7},{8,9},{9,10},{10,11},{11... | collective-permute-start | bytes 4616 | tf_op jit(solution)/shard_map/ppermute | solution.py:19
  280.7 1.5 scatter_custom_fusion.6
  282.2 1.5 scatter_custom_fusion.7
  283.7 1.5 scatter_custom_fusion.8
  285.5 1.7 scatter_custom_fusion.9
  287.4 7.8 %fusion.2 = f32[1,400,1]{1,0,2:T(1,128)S(1)} fusion(f32[3,1280,1]{1,2,0:T(1,128)S(1)} %copy.42, f32[3,400,1,1280]{3,2,1,0:T(1,128)} %param.9), kind=kOutput, calls=%fused_computation.22 | convolution fusion | flops 18432000 | bytes 6160960 | tf_op jit(solution)/shard_map/ckn,cn->k/dot_general | solution.py:74
  295.2 45.3 %psum.15 = f32[400]{0:T(512)S(1)} all-reduce(f32[400]{0:T(512)S(1)} %bitcast.210), channel_id=1, replica_groups=mesh['gx'=4,'gy'=8] {'gx','gy'}, use_global_device_ids=true, to_apply=%region_11.0 | all-reduce | flops 400 | bytes 3200 | tf_op jit(solution)/shard_map/psum | solution.py:40
  341.0 5.7 %fusion = f32[1,3,1280]{2,0,1:T(1,128)S(1)} fusion(f32[400,1,1]{0,1,2:T(1,128)S(1)} %bitcast.208, f32[3,400,1,1280]{3,2,1,0:T(1,128)} %param.9), kind=kOutput, calls=%fused_computation.20 | convolution fusion | flops 18432000 | bytes 6160960 | tf_op jit(solution)/shard_map/ckn,k->cn/dot_general | solution.py:76
  (79 shorter events, 21.5 us)
Async XLA Ops:
  0.6 54.3 %copy-start = (f32[24,24]{1,0:T(8,128)S(1)}, f32[24,24]{1,0:T(8,128)}, u32[]{:S(2)}) copy-start(f32[24,24]{1,0:T(8,128)} %param.14) | copy-start | bytes 6916
  0.6 18.9 %copy-start.1 = (s32[8,1,1024]{2,1,0:T(1,128)S(1)}, s32[8,1,1024]{2,1,0:T(1,128)}, u32[]{:S(2)}) copy-start(s32[8,1,1024]{2,1,0:T(1,128)} %param.10) | copy-start | bytes 98308
  0.7 18.9 %copy-start.8 = (f32[1,1024]{1,0:T(1,128)S(1)}, f32[1,1024]{1,0:T(1,128)}, u32[]{:S(2)}) copy-start(f32[1,1024]{1,0:T(1,128)} %param.13) | copy-start | bytes 12292
  0.7 18.9 %copy-start.7 = (f32[1,1024]{1,0:T(1,128)S(1)}, f32[1,1024]{1,0:T(1,128)}, u32[]{:S(2)}) copy-start(f32[1,1024]{1,0:T(1,128)} %param.12) | copy-start | bytes 12292
  8.3 11.3 %collective-permute-start = (f32[1,3,128]{1,2,0:T(8,128)S(1)}, f32[1,3,128]{1,2,0:T(8,128)S(1)}, u32[]{:S(2)}, u32[]{:S(2)}) collective-permute-start(f32[1,3,128]{1,2,0:T(8,128)S(1)} %bitcast.213), channel_id=1, source_target_pairs={{0,8},{8,16},{16,24},{1,9},{9,17},{17,25},{2,10},{10,18},{18,26},{... | collective-permute-start | bytes 4616 | tf_op jit(solution)/shard_map/ppermute | solution.py:19
  11.4 8.3 %collective-permute-start.1 = (f32[1,3,128]{1,2,0:T(8,128)S(1)}, f32[1,3,128]{1,2,0:T(8,128)S(1)}, u32[]{:S(2)}, u32[]{:S(2)}) collective-permute-start(f32[1,3,128]{1,2,0:T(8,128)S(1)} %bitcast.212), channel_id=1, source_target_pairs={{8,0},{16,8},{24,16},{9,1},{17,9},{25,17},{10,2},{18,10},{26,18},{... | collective-permute-start | bytes 4616 | tf_op jit(solution)/shard_map/ppermute | solution.py:20
  13.3 6.4 %collective-permute-start.2 = (f32[1,3,128]{1,2,0:T(8,128)S(1)}, f32[1,3,128]{1,2,0:T(8,128)S(1)}, u32[]{:S(2)}, u32[]{:S(2)}) collective-permute-start(f32[1,3,128]{1,2,0:T(8,128)S(1)} %bitcast.216), channel_id=1, source_target_pairs={{0,1},{1,2},{2,3},{3,4},{4,5},{5,6},{6,7},{8,9},{9,10},{10,11},{11... | collective-permute-start | bytes 4616 | tf_op jit(solution)/shard_map/ppermute | solution.py:19
  18.2 6.2 %collective-permute-start.3 = (f32[1,3,128]{1,2,0:T(8,128)S(1)}, f32[1,3,128]{1,2,0:T(8,128)S(1)}, u32[]{:S(2)}, u32[]{:S(2)}) collective-permute-start(f32[1,3,128]{1,2,0:T(8,128)S(1)} %bitcast.214), channel_id=1, source_target_pairs={{1,0},{2,1},{3,2},{4,3},{5,4},{6,5},{7,6},{9,8},{10,9},{11,10},{12... | collective-permute-start | bytes 4616 | tf_op jit(solution)/shard_map/ppermute | solution.py:20
  57.8 114.3 %copy-start.2 = (f32[400]{0:T(512)S(1)}, f32[400]{0:T(512)}, u32[]{:S(2)}) copy-start(f32[400]{0:T(512)} %param.15) | copy-start | bytes 4804
  57.8 114.3 %copy-start.4 = (f32[400]{0:T(512)S(1)}, f32[400]{0:T(512)}, u32[]{:S(2)}) copy-start(f32[400]{0:T(512)} %param.16) | copy-start | bytes 4804
  57.8 114.3 %copy-start.5 = (f32[400]{0:T(512)S(1)}, f32[400]{0:T(512)}, u32[]{:S(2)}) copy-start(f32[400]{0:T(512)} %param.17) | copy-start | bytes 4804
  102.4 9.9 %collective-permute-start.4 = (f32[1,3,128]{1,2,0:T(8,128)S(1)}, f32[1,3,128]{1,2,0:T(8,128)S(1)}, u32[]{:S(2)}, u32[]{:S(2)}) collective-permute-start(f32[1,3,128]{1,2,0:T(8,128)S(1)} %get-tuple-element.13), channel_id=1, source_target_pairs={{0,8},{8,16},{16,24},{1,9},{9,17},{17,25},{2,10},{10,18},{18,26},{... | collective-permute-start | bytes 4616 | tf_op jit(solution)/shard_map/ppermute | solution.py:19
  105.3 8.5 %collective-permute-start.5 = (f32[1,3,128]{1,2,0:T(8,128)S(1)}, f32[1,3,128]{1,2,0:T(8,128)S(1)}, u32[]{:S(2)}, u32[]{:S(2)}) collective-permute-start(f32[1,3,128]{1,2,0:T(8,128)S(1)} %get-tuple-element.12), channel_id=1, source_target_pairs={{8,0},{16,8},{24,16},{9,1},{17,9},{25,17},{10,2},{18,10},{26,18},{... | collective-permute-start | bytes 4616 | tf_op jit(solution)/shard_map/ppermute | solution.py:20
  106.6 8.8 %collective-permute-start.6 = (f32[1,3,128]{1,2,0:T(8,128)S(1)}, f32[1,3,128]{1,2,0:T(8,128)S(1)}, u32[]{:S(2)}, u32[]{:S(2)}) collective-permute-start(f32[1,3,128]{1,2,0:T(8,128)S(1)} %get-tuple-element.11), channel_id=1, source_target_pairs={{0,1},{1,2},{2,3},{3,4},{4,5},{5,6},{6,7},{8,9},{9,10},{10,11},{11... | collective-permute-start | bytes 4616 | tf_op jit(solution)/shard_map/ppermute | solution.py:19
  110.9 6.2 %collective-permute-start.7 = (f32[1,3,128]{1,2,0:T(8,128)S(1)}, f32[1,3,128]{1,2,0:T(8,128)S(1)}, u32[]{:S(2)}, u32[]{:S(2)}) collective-permute-start(f32[1,3,128]{1,2,0:T(8,128)S(1)} %get-tuple-element.10), channel_id=1, source_target_pairs={{1,0},{2,1},{3,2},{4,3},{5,4},{6,5},{7,6},{9,8},{10,9},{11,10},{12... | collective-permute-start | bytes 4616 | tf_op jit(solution)/shard_map/ppermute | solution.py:20
  178.7 10.1 %collective-permute-start.8 = (f32[1,3,128]{1,2,0:T(8,128)S(1)}, f32[1,3,128]{1,2,0:T(8,128)S(1)}, u32[]{:S(2)}, u32[]{:S(2)}) collective-permute-start(f32[1,3,128]{1,2,0:T(8,128)S(1)} %bitcast.217), channel_id=1, source_target_pairs={{0,8},{8,16},{16,24},{1,9},{9,17},{17,25},{2,10},{10,18},{18,26},{... | collective-permute-start | bytes 4616 | tf_op jit(solution)/shard_map/ppermute | solution.py:19
  182.0 6.8 %collective-permute-start.9 = (f32[1,3,128]{1,2,0:T(8,128)S(1)}, f32[1,3,128]{1,2,0:T(8,128)S(1)}, u32[]{:S(2)}, u32[]{:S(2)}) collective-permute-start(f32[1,3,128]{1,2,0:T(8,128)S(1)} %bitcast.218), channel_id=1, source_target_pairs={{8,0},{16,8},{24,16},{9,1},{17,9},{25,17},{10,2},{18,10},{26,18},{... | collective-permute-start | bytes 4616 | tf_op jit(solution)/shard_map/ppermute | solution.py:20
  183.3 6.1 %collective-permute-start.10 = (f32[1,3,128]{1,2,0:T(8,128)S(1)}, f32[1,3,128]{1,2,0:T(8,128)S(1)}, u32[]{:S(2)}, u32[]{:S(2)}) collective-permute-start(f32[1,3,128]{1,2,0:T(8,128)S(1)} %bitcast.215), channel_id=1, source_target_pairs={{0,1},{1,2},{2,3},{3,4},{4,5},{5,6},{6,7},{8,9},{9,10},{10,11},{11... | collective-permute-start | bytes 4616 | tf_op jit(solution)/shard_map/ppermute | solution.py:19
  187.5 6.2 %collective-permute-start.11 = (f32[1,3,128]{1,2,0:T(8,128)S(1)}, f32[1,3,128]{1,2,0:T(8,128)S(1)}, u32[]{:S(2)}, u32[]{:S(2)}) collective-permute-start(f32[1,3,128]{1,2,0:T(8,128)S(1)} %bitcast.211), channel_id=1, source_target_pairs={{1,0},{2,1},{3,2},{4,3},{5,4},{6,5},{7,6},{9,8},{10,9},{11,10},{12... | collective-permute-start | bytes 4616 | tf_op jit(solution)/shard_map/ppermute | solution.py:20
  271.7 9.0 %collective-permute-start.12 = (f32[1,3,128]{1,2,0:T(8,128)S(1)}, f32[1,3,128]{1,2,0:T(8,128)S(1)}, u32[]{:S(2)}, u32[]{:S(2)}) collective-permute-start(f32[1,3,128]{1,2,0:T(8,128)S(1)} %get-tuple-element.9), channel_id=1, source_target_pairs={{0,8},{8,16},{16,24},{1,9},{9,17},{17,25},{2,10},{10,18},{18,26},{... | collective-permute-start | bytes 4616 | tf_op jit(solution)/shard_map/ppermute | solution.py:19
  274.1 8.1 %collective-permute-start.13 = (f32[1,3,128]{1,2,0:T(8,128)S(1)}, f32[1,3,128]{1,2,0:T(8,128)S(1)}, u32[]{:S(2)}, u32[]{:S(2)}) collective-permute-start(f32[1,3,128]{1,2,0:T(8,128)S(1)} %get-tuple-element.8), channel_id=1, source_target_pairs={{8,0},{16,8},{24,16},{9,1},{17,9},{25,17},{10,2},{18,10},{26,18},{... | collective-permute-start | bytes 4616 | tf_op jit(solution)/shard_map/ppermute | solution.py:20
  275.4 8.3 %collective-permute-start.14 = (f32[1,3,128]{1,2,0:T(8,128)S(1)}, f32[1,3,128]{1,2,0:T(8,128)S(1)}, u32[]{:S(2)}, u32[]{:S(2)}) collective-permute-start(f32[1,3,128]{1,2,0:T(8,128)S(1)} %get-tuple-element.7), channel_id=1, source_target_pairs={{0,1},{1,2},{2,3},{3,4},{4,5},{5,6},{6,7},{8,9},{9,10},{10,11},{11... | collective-permute-start | bytes 4616 | tf_op jit(solution)/shard_map/ppermute | solution.py:19
  279.3 6.2 %collective-permute-start.15 = (f32[1,3,128]{1,2,0:T(8,128)S(1)}, f32[1,3,128]{1,2,0:T(8,128)S(1)}, u32[]{:S(2)}, u32[]{:S(2)}) collective-permute-start(f32[1,3,128]{1,2,0:T(8,128)S(1)} %get-tuple-element.6), channel_id=1, source_target_pairs={{1,0},{2,1},{3,2},{4,3},{5,4},{6,5},{7,6},{9,8},{10,9},{11,10},{12... | collective-permute-start | bytes 4616 | tf_op jit(solution)/shard_map/ppermute | solution.py:20
  340.5 6.9 %copy-start.6 = (f32[400]{0:T(512)}, f32[400]{0:T(512)S(1)}, u32[]{:S(2)}) copy-start(f32[400]{0:T(512)S(1)} %psum.15) | copy-start | bytes 4804
  341.0 6.3 %copy-start.3 = (f32[400]{0:T(512)}, f32[400]{0:T(512)S(1)}, u32[]{:S(2)}) copy-start(f32[400]{0:T(512)S(1)} %get-tuple-element.4) | copy-start | bytes 4804
where the time goes:
time: 348 us; the launch traced here: 347 us
  other arithmetic  103 us (30%)
  blocking collectives  90.6 us (26%)
  local copies, waits for them, and re-layouts  73.5 us (21%)
  starting transfers between devices  36 us (10%)
  matrix products  33.3 us (10%)
  waiting for transfers between devices  9.93 us (3%)
    psum x2, blocking collectives, advance(): reduced = lax.psum(partial_value, ('gx', 'gy'))  90.6 us
    scatter-add x2, other arithmetic, element_forces(): jnp.zeros_like(moved).at[:, links].add(forces.reshape(3, 8, links.shape[1]))  89.1 us
    gather x4, local copies, waits for them, and re-layouts, element_forces(): corner = moved[:, links]  61.1 us
    ppermute x8, starting transfers between devices, with_halo(): before = lax.ppermute(last, axis, up)  25.7 us
    dot_general x2, matrix products, shards(): jnp.einsum('ckn,cn->k', owned_rows, owned_force, precision=highest)  15.5 us
    scatter-add x8, other arithmetic, shards(): owned_force = owned_force.at[:, senders[side]].add(returned[side])  12.5 us
    dot_general x2, matrix products, shards(): moved_own = jnp.einsum('ckn,k->cn', owned_rows, coords, precision=highest)  11.7 us
    ppermute x8, starting transfers between devices, with_halo(): after = lax.ppermute(first, axis, down)  10.3 us
  transfers between devices with their start and end apart: 16, of which 5 were waited for; matrix products, arithmetic and copies ran while one was open for 4% of the time, Pallas kernels for 0%

commit v1 on v0

v1 whole, which is shorter than its diff:
```python
import functools

import jax
import jax.numpy as jnp
from jax import lax
from jax.experimental import pallas as pl
from jax.experimental.pallas import tpu as pltpu
from jax.sharding import PartitionSpec as P

STEPS = 2
LANES = 128
SUB = 8

time_step = 0.05

MESH = pl.DeviceIdType.MESH


def split(x):
    high = x.astype(jnp.bfloat16).astype(jnp.float32)
    return high, x - high


def kernel(
    sizes,
    basis_hbm,
    links_ref,
    senders_ref,
    modulus_ref,
    weight_ref,
    stiffness_ref,
    coords_ref,
    velocity_ref,
    external_ref,
    coords_out,
    velocity_out,
    reduced_out,
    displaced_out,
    raw,
    phi,
    column,
    vectors,
    table,
    factor,
    forces,
    left_hand,
    right_hand,
    left_back,
    right_back,
    own_force,
    send_u,
    recv_u,
    send_f,
    recv_f,
    sum_x,
    sum_y,
    load_sem,
    u_send_sem,
    u_recv_sem,
    f_send_sem,
    f_recv_sem,
    x_send_sem,
    x_recv_sem,
    y_send_sem,
    y_recv_sem,
):
    modes, tiles, corners, chunks, n_x, n_y = sizes
    blocks = pl.cdiv(modes, LANES)
    table_rows = table.shape[1]
    ix = lax.axis_index("gx")
    iy = lax.axis_index("gy")

    loads = [
        pltpu.make_async_copy(
            basis_hbm.at[pl.ds(c * modes * tiles, modes * tiles), :], raw.at[c], load_sem.at[c]
        )
        for c in range(3)
    ]
    for load in loads:
        load.start()

    recv_u[...] = jnp.zeros_like(recv_u)
    recv_f[...] = jnp.zeros_like(recv_f)
    send_u[...] = jnp.zeros_like(send_u)
    send_f[...] = jnp.zeros_like(send_f)
    sum_x[...] = jnp.zeros_like(sum_x)
    sum_y[...] = jnp.zeros_like(sum_y)

    barrier = pltpu.get_barrier_semaphore()
    for d in range(1, n_x):
        pl.semaphore_signal(
            barrier, inc=1, device_id={"gx": lax.rem(ix + d, n_x)}, device_id_type=MESH
        )
    for d in range(1, n_y):
        pl.semaphore_signal(
            barrier, inc=1, device_id={"gy": lax.rem(iy + d, n_y)}, device_id_type=MESH
        )

    neighbours = [
        (ix > 0, {"gx": lax.rem(ix + n_x - 1, n_x)}),
        (ix < n_x - 1, {"gx": lax.rem(ix + 1, n_x)}),
        (iy > 0, {"gy": lax.rem(iy + n_y - 1, n_y)}),
        (iy < n_y - 1, {"gy": lax.rem(iy + 1, n_y)}),
    ]

    vectors[...] = jnp.zeros_like(vectors)
    for place, ref in enumerate((coords_ref, velocity_ref, external_ref)):
        for j in range(blocks):
            width = min(LANES, modes - j * LANES)
            vectors[place, j : j + 1, :width] = ref[:, j * LANES : j * LANES + width]

    lane = lax.broadcasted_iota(jnp.int32, (LANES, LANES), 1)
    sublane = lax.broadcasted_iota(jnp.int32, (LANES, LANES), 0)
    eye = lane == sublane

    def spread_coords():
        for j in range(blocks):
            height = min(LANES, modes - j * LANES)
            row = jnp.broadcast_to(vectors[0, j : j + 1, :], (height, LANES))
            picked = jnp.where(eye[:height], row, 0.0)
            column[j * LANES : j * LANES + height, :] = jnp.broadcast_to(
                jnp.sum(picked, axis=1, keepdims=True), (height, LANES)
            )

    def fold(product):
        parts = [product[SUB * i : SUB * (i + 1)] for i in range(modes // SUB)]
        while len(parts) > 1:
            nxt = [parts[i] + parts[i + 1] for i in range(0, len(parts) - 1, 2)]
            if len(parts) % 2:
                nxt.append(parts[-1])
            parts = nxt
        return jnp.sum(parts[0], axis=0, keepdims=True)

    def move_tile(t, c):
        rows = raw[c, pl.ds(t, modes, stride=tiles), :]
        phi[c, t] = rows
        table[c, pl.ds(t, 1), :] = fold(rows * column[:modes, :])

    def displace(t):
        spread = column[:modes, :]
        for c in range(3):
            table[c, pl.ds(t, 1), :] = fold(phi[c, t] * spread)

    low_rows = sublane
    factor[...] = modulus_ref[...] * weight_ref[...]
    for chunk in range(corners * chunks):
        low = jnp.broadcast_to(links_ref[chunk : chunk + 1, :] & (LANES - 1), (LANES, LANES))
        right_hand[:, chunk * LANES : (chunk + 1) * LANES] = jnp.where(
            low == low_rows, 1.0, 0.0
        ).astype(jnp.bfloat16)
    for side in range(4):
        low = jnp.broadcast_to(senders_ref[side : side + 1, :] & (LANES - 1), (LANES, LANES))
        right_back[:, side * LANES : (side + 1) * LANES] = jnp.where(
            low == low_rows, 1.0, 0.0
        ).astype(jnp.bfloat16)
    table[...] = jnp.zeros_like(table)
    spread_coords()

    for c in range(3):
        loads[c].wait()
        pl.loop(0, tiles)(functools.partial(move_tile, c=c))

    pl.semaphore_wait(barrier, n_x + n_y - 2)

    high_rows = lax.broadcasted_iota(jnp.int32, (table_rows, LANES), 0)
    contract = (((1,), (1,)), ((), ()))

    def exchange(step, source, target, send_sem, recv_sem):
        copies = []
        for side, (exists, where) in enumerate(neighbours):
            copies.append(
                pltpu.make_async_remote_copy(
                    src_ref=source.at[step, side],
                    dst_ref=target.at[step, side ^ 1],
                    send_sem=send_sem.at[step, side],
                    recv_sem=recv_sem.at[step, side ^ 1],
                    device_id=where,
                    device_id_type=MESH,
                )
            )
        for side, (exists, where) in enumerate(neighbours):
            pl.when(exists)(copies[side].start)
        for side, (exists, where) in enumerate(neighbours):
            arrived = pltpu.make_async_remote_copy(
                src_ref=source.at[step, side],
                dst_ref=target.at[step, side],
                send_sem=send_sem.at[step, side],
                recv_sem=recv_sem.at[step, side],
                device_id=where,
                device_id_type=MESH,
            )
            pl.when(exists)(arrived.wait_recv)
        return lambda: [
            pl.when(exists)(copies[side].wait_send)
            for side, (exists, where) in enumerate(neighbours)
        ]

    def total(step, slots, axis, me, size, send_sem, recv_sem):
        copies = []
        for d in range(1, size):
            copies.append(
                pltpu.make_async_remote_copy(
                    src_ref=slots.at[step, me],
                    dst_ref=slots.at[step, me],
                    send_sem=send_sem.at[step, d],
                    recv_sem=recv_sem.at[step, me],
                    device_id={axis: lax.rem(me + d, size)},
                    device_id_type=MESH,
                )
            )
            copies[-1].start()
        for d in range(1, size):
            other = lax.rem(me + d, size)
            pltpu.make_async_remote_copy(
                src_ref=slots.at[step, other],
                dst_ref=slots.at[step, other],
                send_sem=send_sem.at[step, d],
                recv_sem=recv_sem.at[step, other],
                device_id={axis: other},
                device_id_type=MESH,
            ).wait_recv()
        value = slots[step, 0]
        for i in range(1, size):
            value = value + slots[step, i]
        return value, lambda: [copy.wait_send() for copy in copies]

    def gather(index, rows):
        low = index & (LANES - 1)
        high = lax.shift_right_logical(index, 7)
        found = [jnp.zeros(index.shape, jnp.float32) for _ in range(3)]
        for r in range(rows):
            here = high == r
            for c in range(3):
                row = jnp.broadcast_to(table[c, r : r + 1, :], index.shape)
                taken = jnp.take_along_axis(row, low, axis=1, mode="promise_in_bounds")
                found[c] = jnp.where(here, taken, found[c])
        return found

    senders = jnp.concatenate([senders_ref[...], jnp.zeros((4, LANES), jnp.int32)], axis=0)

    def place(target, chunk, index, values):
        here = jnp.broadcast_to(lax.shift_right_logical(index, 7), high_rows.shape) == high_rows
        for i, value in enumerate(values):
            target[i * table_rows : (i + 1) * table_rows, chunk * LANES : (chunk + 1) * LANES] = (
                jnp.where(here, jnp.broadcast_to(value, high_rows.shape), 0.0).astype(jnp.bfloat16)
            )

    def advance(step):
        for c, found in enumerate(gather(senders, tiles)):
            for side in range(4):
                send_u[step, side, c : c + 1, :] = found[side : side + 1, :]
        sent_u = exchange(step, send_u, recv_u, u_send_sem, u_recv_sem)
        for side in range(4):
            for c in range(3):
                table[c, tiles + side : tiles + side + 1, :] = recv_u[step, side, c : c + 1, :]

        moved = [None] * (3 * corners)
        for q in range(corners):
            index = links_ref[q * chunks : (q + 1) * chunks, :]
            for c, found in enumerate(gather(index, tiles + 4)):
                moved[c * corners + q] = found
        for i in range(3 * corners):
            strain = stiffness_ref[i, 0] * moved[0]
            for j in range(1, 3 * corners):
                strain = strain + stiffness_ref[i, j] * moved[j]
            force = factor[...] * (strain + strain * strain * strain * (1.0 / 3.0))
            high, low = split(force)
            forces[0, i] = high
            forces[1, i] = low
        for q in range(corners):
            for s in range(chunks):
                chunk = q * chunks + s
                place(
                    left_hand,
                    chunk,
                    links_ref[chunk : chunk + 1, :],
                    [
                        forces[h, c * corners + q, s : s + 1, :]
                        for c in range(3)
                        for h in range(2)
                    ],
                )
        nodal = lax.dot_general(
            left_hand[...], right_hand[...], contract, preferred_element_type=jnp.float32
        )
        for c in range(3):
            base = 2 * c * table_rows
            both = nodal[base : base + table_rows] + nodal[base + table_rows : base + 2 * table_rows]
            own_force[c] = both
            for side in range(4):
                send_f[step, side, c : c + 1, :] = both[tiles + side : tiles + side + 1]
        sent_f = exchange(step, send_f, recv_f, f_send_sem, f_recv_sem)
        for side in range(4):
            values = []
            for c in range(3):
                values.extend(split(recv_f[step, side, c : c + 1, :]))
            place(left_back, side, senders_ref[side : side + 1, :], values)
        back = lax.dot_general(
            left_back[...], right_back[...], contract, preferred_element_type=jnp.float32
        )
        for c in range(3):
            base = 2 * c * table_rows
            own_force[c] = (
                own_force[c]
                + back[base : base + table_rows]
                + back[base + table_rows : base + 2 * table_rows]
            )

        height = 5 * SUB if modes % (5 * SUB) == 0 else SUB

        @pl.loop(0, modes // height)
        def _(b):
            rows = pl.ds(pl.multiple_of(b * height, SUB), height)
            acc = [None] * 3
            for c in range(3):
                for t in range(tiles):
                    term = phi[c, t, rows, :] * jnp.broadcast_to(
                        own_force[c, t : t + 1, :], (height, LANES)
                    )
                    acc[c] = term if acc[c] is None else acc[c] + term
            column[rows, :] = jnp.broadcast_to(
                jnp.sum(acc[0] + acc[1] + acc[2], axis=1, keepdims=True), (height, LANES)
            )

        for j in range(blocks):
            rows = min(LANES, modes - j * LANES)
            picked = jnp.where(eye[:rows], column[j * LANES : j * LANES + rows, :], 0.0)
            sum_x[step, ix, j : j + 1, :] = jnp.sum(picked, axis=0, keepdims=True)
        along_x, sent_x = total(step, sum_x, "gx", ix, n_x, x_send_sem, x_recv_sem)
        sum_y[step, iy] = along_x
        reduced, sent_y = total(step, sum_y, "gy", iy, n_y, y_send_sem, y_recv_sem)
        velocity = vectors[1] + time_step * (vectors[2] - reduced)
        vectors[3] = reduced
        vectors[1] = velocity
        vectors[0] = vectors[0] + time_step * velocity
        spread_coords()
        pl.loop(0, tiles)(displace)
        sent_u()
        sent_f()
        sent_x()
        sent_y()

    pl.loop(0, STEPS)(advance)

    for slot, ref in ((0, coords_out), (1, velocity_out), (3, reduced_out)):
        for j in range(blocks):
            width = min(LANES, modes - j * LANES)
            ref[:, j * LANES : j * LANES + width] = vectors[slot, j : j + 1, :width]
    for c in range(3):
        displaced_out[c * tiles : (c + 1) * tiles, :] = table[c, :tiles, :]


def shards(
    basis, connectivity, send_nodes, modulus, ecsw_weight, stiffness, coords, velocity, external
):
    modes, nodes = basis.shape[1], basis.shape[3]
    corners, elements = connectivity.shape[0], connectivity.shape[2]
    tiles, chunks = nodes // LANES, elements // LANES
    n_x, n_y = lax.axis_size("gx"), lax.axis_size("gy")
    blocks = pl.cdiv(modes, LANES)
    table_rows = pl.cdiv(tiles + 4, 16) * 16
    f32 = jnp.float32
    vmem = pl.BlockSpec(memory_space=pltpu.VMEM)
    tile = (SUB, LANES)
    dma = pltpu.SemaphoreType.DMA
    outs = pl.pallas_call(
        functools.partial(kernel, (modes, tiles, corners, chunks, n_x, n_y)),
        out_shape=[jax.ShapeDtypeStruct((1, modes), f32)] * 3
        + [jax.ShapeDtypeStruct((3 * tiles, LANES), f32)],
        in_specs=[pl.BlockSpec(memory_space=pl.ANY)]
        + [vmem] * 4
        + [pl.BlockSpec(memory_space=pltpu.SMEM)]
        + [vmem] * 3,
        out_specs=[vmem] * 4,
        scratch_shapes=[
            pltpu.VMEM((3, modes * tiles, LANES), f32),
            pltpu.VMEM((3, tiles, modes, LANES), f32),
            pltpu.VMEM((blocks * LANES, LANES), f32),
            pltpu.VMEM((4,) + tile, f32),
            pltpu.VMEM((3, table_rows, LANES), f32),
            pltpu.VMEM((chunks, LANES), f32),
            pltpu.VMEM((2, 3 * corners, chunks, LANES), f32),
            pltpu.VMEM((6 * table_rows, corners * elements), jnp.bfloat16),
            pltpu.VMEM((LANES, corners * elements), jnp.bfloat16),
            pltpu.VMEM((6 * table_rows, 4 * LANES), jnp.bfloat16),
            pltpu.VMEM((LANES, 4 * LANES), jnp.bfloat16),
            pltpu.VMEM((3, table_rows, LANES), f32),
            pltpu.VMEM((STEPS, 4) + tile, f32),
            pltpu.VMEM((STEPS, 4) + tile, f32),
            pltpu.VMEM((STEPS, 4) + tile, f32),
            pltpu.VMEM((STEPS, 4) + tile, f32),
            pltpu.VMEM((STEPS, n_x) + tile, f32),
            pltpu.VMEM((STEPS, n_y) + tile, f32),
            dma((3,)),
            dma((STEPS, 4)),
            dma((STEPS, 4)),
            dma((STEPS, 4)),
            dma((STEPS, 4)),
            dma((STEPS, n_x)),
            dma((STEPS, n_x)),
            dma((STEPS, n_y)),
            dma((STEPS, n_y)),
        ],
        compiler_params=pltpu.CompilerParams(collective_id=0, has_side_effects=True),
    )(
        basis.reshape(3 * modes * tiles, LANES),
        connectivity.reshape(corners * chunks, LANES),
        send_nodes.reshape(4, LANES),
        modulus.reshape(chunks, LANES),
        ecsw_weight.reshape(chunks, LANES),
        stiffness,
        coords.reshape(1, modes),
        velocity.reshape(1, modes),
        external.reshape(1, modes),
    )
    coords, velocity, reduced, displaced = outs
    return (
        coords.reshape(modes),
        velocity.reshape(modes),
        reduced.reshape(modes),
        displaced.reshape(3, 1, nodes),
    )


def solution(mesh):
    return jax.shard_map(
        shards,
        mesh=mesh,
        in_specs=(
            P(None, None, "gx", "gy"),
            P(None, "gx", "gy"),
            P(None, "gx", "gy"),
            P("gx", "gy"),
            P("gx", "gy"),
            P(),
            P(),
            P(),
            P(),
        ),
        out_specs=(P(), P(), P(), P(None, "gx", "gy")),
        check_vma=False,
    )
```

time: 348 us -> 48.2 us (0.14)
  other arithmetic: 103 us -> 0 us
  blocking collectives: 90.6 us -> 0 us
  local copies, waits for them, and re-layouts: 73.5 us -> 5.04 us
  Pallas kernels: 0 us -> 42.2 us
  starting transfers between devices: 36 us -> 0 us
  matrix products: 33.3 us -> 0 us
  waiting for transfers between devices: 9.93 us -> 0 us
    scatter-add x10 -> x0, other arithmetic: 102 us -> none  [the longest x2 89.1 us: element_forces(): jnp.zeros_like(moved).at[:, links].add(forces.reshape(3, 8, links.shape[1]))]
    psum x2 -> x0, blocking collectives: 90.6 us -> none  [advance(): reduced = lax.psum(partial_value, ('gx', 'gy'))]
    gather x12 -> x0, local copies, waits for them, and re-layouts: 66.2 us -> none  [the longest x4 61.1 us: element_forces(): corner = moved[:, links]]
    pallas_call x0 -> x1, Pallas kernels: none -> 42.2 us  [shards(): pl.pallas_call(functools.partial(kernel, (modes, tiles, corners, chunks,...]
    ppermute x16 -> x0, starting transfers between devices: 36 us -> none  [the longest x8 25.7 us: with_halo(): before = lax.ppermute(last, axis, up)]
    dot_general x7 -> x0, matrix products: 33.3 us -> none  [the longest x2 15.5 us: shards(): jnp.einsum('ckn,cn->k', owned_rows, owned_force, precision=highest)]
    ppermute x16 -> x0, waiting for transfers between devices: 9.93 us -> none  [the longest x8 9.37 us: with_halo(): after = lax.ppermute(first, axis, down)]
    reshape x2 -> x1, local copies, waits for them, and re-layouts: 5.3 us -> 1.33 us  [shards(): displaced.reshape(3, 1, nodes)]
  transfers between devices with their start and end apart: 16 -> 0, of which waited for: 5 -> 0; matrix products, arithmetic and copies ran while one was open for 4% -> 0% of each run, Pallas kernels for 0% -> 0%
where the time goes in v1:
time: 48.2 us; the launch traced here: 47.9 us
  Pallas kernels  42.2 us (88%)
  local copies, waits for them, and re-layouts  5.04 us (10%)
  between operations  0.64 us (1%)
    pallas_call x1, Pallas kernels, shards(): pl.pallas_call(functools.partial(kernel, (modes, tiles, corners, chunks,...  42.2 us
    unnamed x3, local copies, waits for them, and re-layouts  3.71 us
    reshape x1, local copies, waits for them, and re-layouts, shards(): displaced.reshape(3, 1, nodes)  1.33 us

profile of v1, /device:TPU:0, one launch (start us, length us, event | category | flops | bytes accessed | tf_op | source)
XLA Modules:
  0.0 47.9 jit_solution(1230628622514733813)
XLA Ops:
  0.6 42.2 %shard_map.120 = (f32[1,400]{1,0:T(1,128)}, f32[1,400]{1,0:T(1,128)}, f32[1,400]{1,0:T(1,128)}, f32[30,128]{1,0:T(8,128)}) custom-call(f32[12000,128]{1,0:T(8,128)} %bitcast.11, s32[64,128]{1,0:T(8,128)} %bitcast.12, s32[4,128]{1,0:T(4,128)} %bitcast.15, f32[8,128]{1,0:T(8,128)} %bitcast.13, f32[8,128]{1,0:T(8,128)} %bitcast.14, f32[24,24]{1,0:T(8,128)} %stiffness_ref.1, ...), custom_call_target="tpu_custom_call" | custom-call | tf_op jit(solution)/shard_map/pallas_call | solution.py:366
  42.8 1.3 %reshape.56 = f32[3,1,1280]{2,1,0:T(1,128)} reshape(f32[30,128]{1,0:T(8,128)} %get-tuple-element.11) | data formatting | bytes 30720 | tf_op jit(solution)/shard_map/reshape | solution.py:421
  44.2 1.2 %copy.18 = f32[400]{0:T(512)} copy(f32[400]{0:T(512)} %bitcast.21) | data formatting | bytes 3200
  45.4 1.2 %copy.19 = f32[400]{0:T(512)} copy(f32[400]{0:T(512)} %bitcast.20) | data formatting | bytes 3200
  46.6 1.2 %copy.20 = f32[400]{0:T(512)} copy(f32[400]{0:T(512)} %bitcast.19) | data formatting | bytes 3200

commit v2 on v1

--- a/solution.py
+++ b/solution.py
@@ -32,16 +32,14 @@
     coords_ref,
     velocity_ref,
     external_ref,
-    coords_out,
-    velocity_out,
-    reduced_out,
-    displaced_out,
+    packed_out,
     raw,
     phi,
     column,
     vectors,
     table,
     factor,
+    moved,
     forces,
     left_hand,
     right_hand,
@@ -66,7 +64,8 @@
 ):
     modes, tiles, corners, chunks, n_x, n_y = sizes
     blocks = pl.cdiv(modes, LANES)
-    table_rows = table.shape[1]
+    groups = own_force.shape[2]
+    wide = right_hand.shape[0]
     ix = lax.axis_index("gx")
     iy = lax.axis_index("gy")
 
@@ -83,8 +82,6 @@
     recv_f[...] = jnp.zeros_like(recv_f)
     send_u[...] = jnp.zeros_like(send_u)
     send_f[...] = jnp.zeros_like(send_f)
-    sum_x[...] = jnp.zeros_like(sum_x)
-    sum_y[...] = jnp.zeros_like(sum_y)
 
     barrier = pltpu.get_barrier_semaphore()
     for d in range(1, n_x):
@@ -141,19 +138,21 @@
         for c in range(3):
             table[c, pl.ds(t, 1), :] = fold(phi[c, t] * spread)
 
-    low_rows = sublane
-    factor[...] = modulus_ref[...] * weight_ref[...]
-    for chunk in range(corners * chunks):
-        low = jnp.broadcast_to(links_ref[chunk : chunk + 1, :] & (LANES - 1), (LANES, LANES))
-        right_hand[:, chunk * LANES : (chunk + 1) * LANES] = jnp.where(
+    low_rows = lax.broadcasted_iota(jnp.int32, (wide, LANES), 0)
+
+    def one_hot(target, chunk, index):
+        low = jnp.broadcast_to(index & (wide - 1), (wide, LANES))
+        target[:, chunk * LANES : (chunk + 1) * LANES] = jnp.where(
             low == low_rows, 1.0, 0.0
         ).astype(jnp.bfloat16)
-    for side in range(4):
-        low = jnp.broadcast_to(senders_ref[side : side + 1, :] & (LANES - 1), (LANES, LANES))
-        right_back[:, side * LANES : (side + 1) * LANES] = jnp.where(
-            low == low_rows, 1.0, 0.0
-        ).astype(jnp.bfloat16)
-    table[...] = jnp.zeros_like(table)
+
+    def prepare():
+        for chunk in range(corners * chunks):
+            one_hot(right_hand, chunk, links_ref[chunk : chunk + 1, :])
+        for side in range(4):
+            one_hot(right_back, side, senders_ref[side : side + 1, :])
+
+    factor[...] = modulus_ref[...] * weight_ref[...]
     spread_coords()
 
     for c in range(3):
@@ -162,7 +161,7 @@
 
     pl.semaphore_wait(barrier, n_x + n_y - 2)
 
-    high_rows = lax.broadcasted_iota(jnp.int32, (table_rows, LANES), 0)
+    high_rows = lax.broadcasted_iota(jnp.int32, (groups, LANES), 0)
     contract = (((1,), (1,)), ((), ()))
 
     def exchange(step, source, target, send_sem, recv_sem):
@@ -180,6 +179,9 @@
             )
         for side, (exists, where) in enumerate(neighbours):
             pl.when(exists)(copies[side].start)
+        return copies
+
+    def arrive(step, source, target, send_sem, recv_sem):
         for side, (exists, where) in enumerate(neighbours):
             arrived = pltpu.make_async_remote_copy(
                 src_ref=source.at[step, side],
@@ -190,10 +192,10 @@
                 device_id_type=MESH,
             )
             pl.when(exists)(arrived.wait_recv)
-        return lambda: [
+
+    def sent(copies):
+        for side, (exists, where) in enumerate(neighbours):
             pl.when(exists)(copies[side].wait_send)
-            for side, (exists, where) in enumerate(neighbours)
-        ]
 
     def total(step, slots, axis, me, size, send_sem, recv_sem):
         copies = []
@@ -224,49 +226,68 @@
             value = value + slots[step, i]
         return value, lambda: [copy.wait_send() for copy in copies]
 
-    def gather(index, rows):
+    def gather(index, rows, found):
         low = index & (LANES - 1)
         high = lax.shift_right_logical(index, 7)
-        found = [jnp.zeros(index.shape, jnp.float32) for _ in range(3)]
-        for r in range(rows):
+        for r, row_of in rows:
             here = high == r
             for c in range(3):
-                row = jnp.broadcast_to(table[c, r : r + 1, :], index.shape)
+                row = jnp.broadcast_to(row_of(c), index.shape)
                 taken = jnp.take_along_axis(row, low, axis=1, mode="promise_in_bounds")
                 found[c] = jnp.where(here, taken, found[c])
         return found
 
+    own_rows = [(r, lambda c, r=r: table[c, r : r + 1, :]) for r in range(tiles)]
     senders = jnp.concatenate([senders_ref[...], jnp.zeros((4, LANES), jnp.int32)], axis=0)
+    zero = jnp.zeros((chunks, LANES), jnp.float32)
 
     def place(target, chunk, index, values):
-        here = jnp.broadcast_to(lax.shift_right_logical(index, 7), high_rows.shape) == high_rows
-        for i, value in enumerate(values):
-            target[i * table_rows : (i + 1) * table_rows, chunk * LANES : (chunk + 1) * LANES] = (
-                jnp.where(here, jnp.broadcast_to(value, high_rows.shape), 0.0).astype(jnp.bfloat16)
-            )
+        here = jnp.broadcast_to(lax.shift_right_logical(index, 8), high_rows.shape) == high_rows
+        for c, pair in enumerate(values):
+            both = [jnp.where(here, jnp.broadcast_to(x, high_rows.shape), 0.0) for x in pair]
+            target[2 * c * groups : 2 * (c + 1) * groups, chunk * LANES : (chunk + 1) * LANES] = (
+                jnp.concatenate(both, axis=0).astype(jnp.bfloat16)
+            )
+
+    def scattered(left, right):
+        product = lax.dot_general(
+            left[...], right[...], contract, preferred_element_type=jnp.float32
+        )
+        return [
+            product[2 * c * groups : (2 * c + 1) * groups]
+            + product[(2 * c + 1) * groups : (2 * c + 2) * groups]
+            for c in range(3)
+        ]
 
     def advance(step):
-        for c, found in enumerate(gather(senders, tiles)):
+        for c, found in enumerate(
+            gather(senders, own_rows, [jnp.zeros((SUB, LANES), jnp.float32)] * 3)
+        ):
             for side in range(4):
                 send_u[step, side, c : c + 1, :] = found[side : side + 1, :]
         sent_u = exchange(step, send_u, recv_u, u_send_sem, u_recv_sem)
-        for side in range(4):
-            for c in range(3):
-                table[c, tiles + side : tiles + side + 1, :] = recv_u[step, side, c : c + 1, :]
-
-        moved = [None] * (3 * corners)
+        pl.when(step == 0)(prepare)
         for q in range(corners):
             index = links_ref[q * chunks : (q + 1) * chunks, :]
-            for c, found in enumerate(gather(index, tiles + 4)):
+            for c, found in enumerate(gather(index, own_rows, [zero] * 3)):
                 moved[c * corners + q] = found
+        arrive(step, send_u, recv_u, u_send_sem, u_recv_sem)
+        edge_rows = [
+            (tiles + side, lambda c, side=side: recv_u[step, side, c : c + 1, :])
+            for side in range(4)
+        ]
+        corner = [None] * (3 * corners)
+        for q in range(corners):
+            index = links_ref[q * chunks : (q + 1) * chunks, :]
+            begun = [moved[c * corners + q] for c in range(3)]
+            for c, found in enumerate(gather(index, edge_rows, begun)):
+                corner[c * corners + q] = found
         for i in range(3 * corners):
-            strain = stiffness_ref[i, 0] * moved[0]
+            strain = stiffness_ref[i, 0] * corner[0]
             for j in range(1, 3 * corners):
-                strain = strain + stiffness_ref[i, j] * moved[j]
+                strain = strain + stiffness_ref[i, j] * corner[j]
             force = factor[...] * (strain + strain * strain * strain * (1.0 / 3.0))
-            high, low = split(force)
-            forces[0, i] = high
-            forces[1, i] = low
+            forces[0, i], forces[1, i] = split(force)
         for q in range(corners):
             for s in range(chunks):
                 chunk = q * chunks + s
@@ -275,36 +296,30 @@
                     chunk,
                     links_ref[chunk : chunk + 1, :],
                     [
-                        forces[h, c * corners + q, s : s + 1, :]
+                        [forces[h, c * corners + q, s : s + 1, :] for h in range(2)]
                         for c in range(3)
-                        for h in range(2)
                     ],
                 )
-        nodal = lax.dot_general(
-            left_hand[...], right_hand[...], contract, preferred_element_type=jnp.float32
-        )
-        for c in range(3):
-            base = 2 * c * table_rows
-            both = nodal[base : base + table_rows] + nodal[base + table_rows : base + 2 * table_rows]
-            own_force[c] = both
+        for c, both in enumerate(scattered(left_hand, right_hand)):
+            for half in range(2):
+                own_force[c, half] = both[:, half * LANES : (half + 1) * LANES]
             for side in range(4):
-                send_f[step, side, c : c + 1, :] = both[tiles + side : tiles + side + 1]
+                row, half = (tiles + side) // 2, (tiles + side) % 2
+                send_f[step, side, c : c + 1, :] = both[
+                    row : row + 1, half * LANES : (half + 1) * LANES
+                ]
         sent_f = exchange(step, send_f, recv_f, f_send_sem, f_recv_sem)
+        arrive(step, send_f, recv_f, f_send_sem, f_recv_sem)
         for side in range(4):
-            values = []
-            for c in range(3):
-                values.extend(split(recv_f[step, side, c : c + 1, :]))
-            place(left_back, side, senders_ref[side : side + 1, :], values)
-        back = lax.dot_general(
-            left_back[...], right_back[...], contract, preferred_element_type=jnp.float32
-        )
-        for c in range(3):
-            base = 2 * c * table_rows
-            own_force[c] = (
-                own_force[c]
-                + back[base : base + table_rows]
-                + back[base + table_rows : base + 2 * table_rows]
-            )
+            place(
+                left_back,
+                side,
+                senders_ref[side : side + 1, :],
+                [split(recv_f[step, side, c : c + 1, :]) for c in range(3)],
+            )
+        for c, both in enumerate(scattered(left_back, right_back)):
+            for half in range(2):
+                own_force[c, half] += both[:, half * LANES : (half + 1) * LANES]
 
         height = 5 * SUB if modes % (5 * SUB) == 0 else SUB
 
@@ -315,7 +330,7 @@
             for c in range(3):
                 for t in range(tiles):
                     term = phi[c, t, rows, :] * jnp.broadcast_to(
-                        own_force[c, t : t + 1, :], (height, LANES)
+                        own_force[c, t % 2, t // 2 : t // 2 + 1, :], (height, LANES)
                     )
                     acc[c] = term if acc[c] is None else acc[c] + term
             column[rows, :] = jnp.broadcast_to(
@@ -335,19 +350,33 @@
         vectors[0] = vectors[0] + time_step * velocity
         spread_coords()
         pl.loop(0, tiles)(displace)
-        sent_u()
-        sent_f()
+        sent(sent_u)
+        sent(sent_f)
         sent_x()
         sent_y()
 
     pl.loop(0, STEPS)(advance)
 
-    for slot, ref in ((0, coords_out), (1, velocity_out), (3, reduced_out)):
+    for place_out, slot in enumerate((0, 1, 3)):
+        packed_out[place_out * blocks : (place_out + 1) * blocks, :] = vectors[slot]
+    for c in range(3):
+        first = 3 * blocks + c * tiles
+        packed_out[first : first + tiles, :] = table[c, :tiles, :]
+
+
+def unpack(packed, coords_out, velocity_out, reduced_out, displaced_out):
+    modes = coords_out.shape[1]
+    blocks = pl.cdiv(modes, LANES)
+    for slot, ref in enumerate((coords_out, velocity_out, reduced_out)):
         for j in range(blocks):
             width = min(LANES, modes - j * LANES)
-            ref[:, j * LANES : j * LANES + width] = vectors[slot, j : j + 1, :width]
+            row = slot * blocks + j
+            ref[:, j * LANES : j * LANES + width] = packed[row : row + 1, :width]
+    tiles = displaced_out.shape[2] // LANES
     for c in range(3):
-        displaced_out[c * tiles : (c + 1) * tiles, :] = table[c, :tiles, :]
+        for t in range(tiles):
+            row = 3 * blocks + c * tiles + t
+            displaced_out[c, :, t * LANES : (t + 1) * LANES] = packed[row : row + 1, :]
 
 
 def shards(
@@ -358,39 +387,40 @@
     tiles, chunks = nodes // LANES, elements // LANES
     n_x, n_y = lax.axis_size("gx"), lax.axis_size("gy")
     blocks = pl.cdiv(modes, LANES)
-    table_rows = pl.cdiv(tiles + 4, 16) * 16
+    groups = pl.cdiv(pl.cdiv(tiles + 4, 2), SUB) * SUB
+    wide = 2 * LANES
     f32 = jnp.float32
     vmem = pl.BlockSpec(memory_space=pltpu.VMEM)
-    tile = (SUB, LANES)
+    tile = (4, LANES)
     dma = pltpu.SemaphoreType.DMA
-    outs = pl.pallas_call(
+    packed = pl.pallas_call(
         functools.partial(kernel, (modes, tiles, corners, chunks, n_x, n_y)),
-        out_shape=[jax.ShapeDtypeStruct((1, modes), f32)] * 3
-        + [jax.ShapeDtypeStruct((3 * tiles, LANES), f32)],
+        out_shape=jax.ShapeDtypeStruct((3 * blocks + 3 * tiles, LANES), f32),
         in_specs=[pl.BlockSpec(memory_space=pl.ANY)]
         + [vmem] * 4
         + [pl.BlockSpec(memory_space=pltpu.SMEM)]
         + [vmem] * 3,
-        out_specs=[vmem] * 4,
+        out_specs=vmem,
         scratch_shapes=[
             pltpu.VMEM((3, modes * tiles, LANES), f32),
             pltpu.VMEM((3, tiles, modes, LANES), f32),
             pltpu.VMEM((blocks * LANES, LANES), f32),
-            pltpu.VMEM((4,) + tile, f32),
-            pltpu.VMEM((3, table_rows, LANES), f32),
+            pltpu.VMEM((4, blocks, LANES), f32),
+            pltpu.VMEM((3, tiles, LANES), f32),
             pltpu.VMEM((chunks, LANES), f32),
+            pltpu.VMEM((3 * corners, chunks, LANES), f32),
             pltpu.VMEM((2, 3 * corners, chunks, LANES), f32),
-            pltpu.VMEM((6 * table_rows, corners * elements), jnp.bfloat16),
-            pltpu.VMEM((LANES, corners * elements), jnp.bfloat16),
-            pltpu.VMEM((6 * table_rows, 4 * LANES), jnp.bfloat16),
-            pltpu.VMEM((LANES, 4 * LANES), jnp.bfloat16),
-            pltpu.VMEM((3, table_rows, LANES), f32),
+            pltpu.VMEM((6 * groups, corners * elements), jnp.bfloat16),
+            pltpu.VMEM((wide, corners * elements), jnp.bfloat16),
+            pltpu.VMEM((6 * groups, 4 * LANES), jnp.bfloat16),
+            pltpu.VMEM((wide, 4 * LANES), jnp.bfloat16),
+            pltpu.VMEM((3, 2, groups, LANES), f32),
             pltpu.VMEM((STEPS, 4) + tile, f32),
             pltpu.VMEM((STEPS, 4) + tile, f32),
             pltpu.VMEM((STEPS, 4) + tile, f32),
             pltpu.VMEM((STEPS, 4) + tile, f32),
-            pltpu.VMEM((STEPS, n_x) + tile, f32),
-            pltpu.VMEM((STEPS, n_y) + tile, f32),
+            pltpu.VMEM((STEPS, n_x, blocks, LANES), f32),
+            pltpu.VMEM((STEPS, n_y, blocks, LANES), f32),
             dma((3,)),
             dma((STEPS, 4)),
             dma((STEPS, 4)),
@@ -413,12 +443,18 @@
         velocity.reshape(1, modes),
         external.reshape(1, modes),
     )
-    coords, velocity, reduced, displaced = outs
+    coords, velocity, reduced, displaced = pl.pallas_call(
+        unpack,
+        out_shape=[jax.ShapeDtypeStruct((1, modes), f32)] * 3
+        + [jax.ShapeDtypeStruct((3, 1, nodes), f32)],
+        in_specs=[vmem],
+        out_specs=[vmem] * 4,
+    )(packed)
     return (
         coords.reshape(modes),
         velocity.reshape(modes),
         reduced.reshape(modes),
-        displaced.reshape(3, 1, nodes),
+        displaced,
     )
 
 

time: 48.2 us -> 43.9 us (0.911)
  local copies, waits for them, and re-layouts: 5.04 us -> 0 us
  Pallas kernels: 42.2 us -> 43 us
    unnamed x3 -> x0, local copies, waits for them, and re-layouts: 3.71 us -> none
    pallas_call x0 -> x1, Pallas kernels: none -> 1.37 us  [shards(): pl.pallas_call(unpack, out_shape=[jax.ShapeDtypeStruct((1, modes), f32)]...]
    reshape x1 -> x0, local copies, waits for them, and re-layouts: 1.33 us -> none  [shards(): displaced.reshape(3, 1, nodes)]
    pallas_call x1, Pallas kernels: 42.2 us -> 41.6 us  [shards(): pl.pallas_call(functools.partial(kernel, (modes, tiles, corners, chunks,...]
where the time goes in v2:
time: 43.9 us; the launch traced here: 43.6 us
  Pallas kernels  43 us (98%)
  between operations  0.64 us (1%)
    pallas_call x1, Pallas kernels, shards(): pl.pallas_call(functools.partial(kernel, (modes, tiles, corners, chunks,...  41.6 us
    pallas_call x1, Pallas kernels, shards(): pl.pallas_call(unpack, out_shape=[jax.ShapeDtypeStruct((1, modes), f32)]...  1.37 us

profile of v2, /device:TPU:0, one launch (start us, length us, event | category | flops | bytes accessed | tf_op | source)
XLA Modules:
  0.0 43.6 jit_solution(5586209945614475294)
XLA Ops:
  0.6 41.6 %shard_map.120.packed = f32[42,128]{1,0:T(8,128)} custom-call(f32[12000,128]{1,0:T(8,128)} %bitcast.11, s32[64,128]{1,0:T(8,128)} %bitcast.12, s32[4,128]{1,0:T(4,128)} %bitcast.15, f32[8,128]{1,0:T(8,128)} %bitcast.13, f32[8,128]{1,0:T(8,128)} %bitcast.14, f32[24,24]{1,0:T(8,128)} %stiffness_ref.1, f32[1,400]{1,0:T(1,128)} %bitcast.16, f32[1,400]{1,0:T(1,128)} %bitcast.17, ...), custom_call_target="tpu_custom_call" | custom-call | tf_op jit(solution)/shard_map/pallas_call | solution.py:396
  42.2 1.4 %shard_map.121 = (f32[1,400]{1,0:T(1,128)}, f32[1,400]{1,0:T(1,128)}, f32[1,400]{1,0:T(1,128)}, f32[3,1,1280]{2,1,0:T(1,128)}) custom-call(f32[42,128]{1,0:T(8,128)} %shard_map.120.packed), custom_call_target="tpu_custom_call" | custom-call | tf_op jit(solution)/shard_map/pallas_call | solution.py:446

commit v3 on v2

--- a/solution.py
+++ b/solution.py
@@ -24,6 +24,15 @@
 def kernel(
     sizes,
     basis_hbm,
+    links_hbm,
+    senders_hbm,
+    modulus_hbm,
+    weight_hbm,
+    stiffness_hbm,
+    coords_hbm,
+    velocity_hbm,
+    external_hbm,
+    packed_out,
     links_ref,
     senders_ref,
     modulus_ref,
@@ -32,7 +41,7 @@
     coords_ref,
     velocity_ref,
     external_ref,
-    packed_out,
+    small_sem,
     raw,
     phi,
     column,
@@ -75,13 +84,8 @@
         )
         for c in range(3)
     ]
-    for load in loads:
-        load.start()
-
     recv_u[...] = jnp.zeros_like(recv_u)
     recv_f[...] = jnp.zeros_like(recv_f)
-    send_u[...] = jnp.zeros_like(send_u)
-    send_f[...] = jnp.zeros_like(send_f)
 
     barrier = pltpu.get_barrier_semaphore()
     for d in range(1, n_x):
@@ -93,6 +97,26 @@
             barrier, inc=1, device_id={"gy": lax.rem(iy + d, n_y)}, device_id_type=MESH
         )
 
+    small = [
+        pltpu.make_async_copy(source, target, small_sem.at[i])
+        for i, (source, target) in enumerate(
+            (
+                (coords_hbm, coords_ref),
+                (velocity_hbm, velocity_ref),
+                (external_hbm, external_ref),
+                (senders_hbm, senders_ref),
+                (links_hbm, links_ref),
+                (modulus_hbm, modulus_ref),
+                (weight_hbm, weight_ref),
+                (stiffness_hbm, stiffness_ref),
+            )
+        )
+    ]
+    for load in small + loads:
+        load.start()
+    send_u[...] = jnp.zeros_like(send_u)
+    send_f[...] = jnp.zeros_like(send_f)
+
     neighbours = [
         (ix > 0, {"gx": lax.rem(ix + n_x - 1, n_x)}),
         (ix < n_x - 1, {"gx": lax.rem(ix + 1, n_x)}),
@@ -101,6 +125,8 @@
     ]
 
     vectors[...] = jnp.zeros_like(vectors)
+    for load in small:
+        load.wait()
     for place, ref in enumerate((coords_ref, velocity_ref, external_ref)):
         for j in range(blocks):
             width = min(LANES, modes - j * LANES)
@@ -396,12 +422,18 @@
     packed = pl.pallas_call(
         functools.partial(kernel, (modes, tiles, corners, chunks, n_x, n_y)),
         out_shape=jax.ShapeDtypeStruct((3 * blocks + 3 * tiles, LANES), f32),
-        in_specs=[pl.BlockSpec(memory_space=pl.ANY)]
-        + [vmem] * 4
-        + [pl.BlockSpec(memory_space=pltpu.SMEM)]
-        + [vmem] * 3,
+        in_specs=[pl.BlockSpec(memory_space=pl.ANY)] * 9,
         out_specs=vmem,
         scratch_shapes=[
+            pltpu.VMEM((corners * chunks, LANES), jnp.int32),
+            pltpu.VMEM((4, LANES), jnp.int32),
+            pltpu.VMEM((chunks, LANES), f32),
+            pltpu.VMEM((chunks, LANES), f32),
+            pltpu.SMEM(stiffness.shape, f32),
+            pltpu.VMEM((1, modes), f32),
+            pltpu.VMEM((1, modes), f32),
+            pltpu.VMEM((1, modes), f32),
+            dma((8,)),
             pltpu.VMEM((3, modes * tiles, LANES), f32),
             pltpu.VMEM((3, tiles, modes, LANES), f32),
             pltpu.VMEM((blocks * LANES, LANES), f32),

time: 43.9 us -> 43 us (0.979)
  Pallas kernels: 43 us -> 42.2 us
    pallas_call x1, Pallas kernels: 41.6 us -> 40.8 us  [shards(): pl.pallas_call(functools.partial(kernel, (modes, tiles, corners, chunks,...]
where the time goes in v3:
time: 43 us; the launch traced here: 42.9 us
  Pallas kernels  42.2 us (98%)
  between operations  0.64 us (1%)
    pallas_call x1, Pallas kernels, shards(): pl.pallas_call(functools.partial(kernel, (modes, tiles, corners, chunks,...  40.8 us
    pallas_call x1, Pallas kernels, shards(): pl.pallas_call(unpack, out_shape=[jax.ShapeDtypeStruct((1, modes), f32)]...  1.37 us

profile of v3, /device:TPU:0, one launch (start us, length us, event | category | flops | bytes accessed | tf_op | source)
XLA Modules:
  0.0 42.9 jit_solution(11215921524517025876)
XLA Ops:
  0.6 40.8 %shard_map.120.packed = f32[42,128]{1,0:T(8,128)} custom-call(f32[12000,128]{1,0:T(8,128)} %bitcast.11, s32[64,128]{1,0:T(8,128)} %bitcast.12, s32[4,128]{1,0:T(4,128)} %bitcast.15, f32[8,128]{1,0:T(8,128)} %bitcast.13, f32[8,128]{1,0:T(8,128)} %bitcast.14, f32[24,24]{1,0:T(8,128)} %stiffness_hbm.1, f32[1,400]{1,0:T(1,128)} %bitcast.16, f32[1,400]{1,0:T(1,128)} %bitcast.17, ...), custom_call_target="tpu_custom_call" | custom-call | tf_op jit(solution)/shard_map/pallas_call | solution.py:422
  41.5 1.4 %shard_map.121 = (f32[1,400]{1,0:T(1,128)}, f32[1,400]{1,0:T(1,128)}, f32[1,400]{1,0:T(1,128)}, f32[3,1,1280]{2,1,0:T(1,128)}) custom-call(f32[42,128]{1,0:T(8,128)} %shard_map.120.packed), custom_call_target="tpu_custom_call" | custom-call | tf_op jit(solution)/shard_map/pallas_call | solution.py:478

commit v4 on v3

--- a/solution.py
+++ b/solution.py
@@ -159,10 +159,23 @@
         phi[c, t] = rows
         table[c, pl.ds(t, 1), :] = fold(rows * column[:modes, :])
 
-    def displace(t):
-        spread = column[:modes, :]
+    group = 2 if tiles % 2 == 0 else 1
+
+    def displace(g):
+        acc = {}
+        for i in range(modes // SUB):
+            rows = slice(SUB * i, SUB * (i + 1))
+            spread = column[rows, :]
+            for c in range(3):
+                for t in range(group):
+                    term = phi[c, g * group + t, rows, :] * spread
+                    key = (c, t, i % 2)
+                    acc[key] = acc[key] + term if key in acc else term
         for c in range(3):
-            table[c, pl.ds(t, 1), :] = fold(phi[c, t] * spread)
+            for t in range(group):
+                table[c, pl.ds(g * group + t, 1), :] = jnp.sum(
+                    acc[c, t, 0] + acc[c, t, 1], axis=0, keepdims=True
+                )
 
     low_rows = lax.broadcasted_iota(jnp.int32, (wide, LANES), 0)
 
@@ -347,7 +360,7 @@
             for half in range(2):
                 own_force[c, half] += both[:, half * LANES : (half + 1) * LANES]
 
-        height = 5 * SUB if modes % (5 * SUB) == 0 else SUB
+        height = 10 * SUB if modes % (10 * SUB) == 0 else SUB
 
         @pl.loop(0, modes // height)
         def _(b):
@@ -375,7 +388,7 @@
         vectors[1] = velocity
         vectors[0] = vectors[0] + time_step * velocity
         spread_coords()
-        pl.loop(0, tiles)(displace)
+        pl.loop(0, tiles // group)(displace)
         sent(sent_u)
         sent(sent_f)
         sent_x()

time: 43 us -> 41.7 us (0.970)
  Pallas kernels: 42.2 us -> 40.8 us
    pallas_call x1, Pallas kernels: 40.8 us -> 39.5 us  [shards(): pl.pallas_call(functools.partial(kernel, (modes, tiles, corners, chunks,...]
where the time goes in v4:
time: 41.7 us; the launch traced here: 41.5 us
  Pallas kernels  40.8 us (98%)
  between operations  0.64 us (2%)
    pallas_call x1, Pallas kernels, shards(): pl.pallas_call(functools.partial(kernel, (modes, tiles, corners, chunks,...  39.5 us
    pallas_call x1, Pallas kernels, shards(): pl.pallas_call(unpack, out_shape=[jax.ShapeDtypeStruct((1, modes), f32)]...  1.37 us

profile of v4, /device:TPU:0, one launch (start us, length us, event | category | flops | bytes accessed | tf_op | source)
XLA Modules:
  0.0 41.5 jit_solution(10747755658572950763)
XLA Ops:
  0.6 39.5 %shard_map.120.packed = f32[42,128]{1,0:T(8,128)} custom-call(f32[12000,128]{1,0:T(8,128)} %bitcast.11, s32[64,128]{1,0:T(8,128)} %bitcast.12, s32[4,128]{1,0:T(4,128)} %bitcast.15, f32[8,128]{1,0:T(8,128)} %bitcast.13, f32[8,128]{1,0:T(8,128)} %bitcast.14, f32[24,24]{1,0:T(8,128)} %stiffness_hbm.1, f32[1,400]{1,0:T(1,128)} %bitcast.16, f32[1,400]{1,0:T(1,128)} %bitcast.17, ...), custom_call_target="tpu_custom_call" | custom-call | tf_op jit(solution)/shard_map/pallas_call | solution.py:435
  40.1 1.4 %shard_map.121 = (f32[1,400]{1,0:T(1,128)}, f32[1,400]{1,0:T(1,128)}, f32[1,400]{1,0:T(1,128)}, f32[3,1,1280]{2,1,0:T(1,128)}) custom-call(f32[42,128]{1,0:T(8,128)} %shard_map.120.packed), custom_call_target="tpu_custom_call" | custom-call | tf_op jit(solution)/shard_map/pallas_call | solution.py:491
